TPU v7x, 32 devices: a whole 2x2x4 slice. The times are simulated.
32 devices in a mesh: tile: 8 (over z, y), cplx: 4 (over x, core).
Axes of the slice: x: 2, y: 2, z: 4, core: 2. Of those that a mesh axis runs over, the one named last changes fastest.
Arguments:
- pair_tiles: bfloat16 [96, 128, 128, 128], P(('tile', 'cplx'))
- tile_map: int32 [96, 3], replicated, may hold values from -1 to 3, as said below
- lengths: int32 [4], replicated, may hold values from 256 to 512
- resolved: int32 [4, 512], replicated, may hold values 0 or 1
- ln_gain: float32 [128], replicated, may hold values from 0.1 to 1.9
- w_in: bfloat16 [128, 512], replicated, may hold values from -0.5 to 0.5
- w_out: bfloat16 [512, 128], replicated, may hold values from -0.25 to 0.25
- w_head: bfloat16 [128, 64], replicated
- head_bias: float32 [64], replicated, may hold values from -4 to 4
Outputs:
- error_map: float32 [4, 512, 512], P('cplx', 'tile')
- residue_error: float32 [4, 512], P('cplx', 'tile')
- tm_score: float32 [4], P('cplx')
Inputs may be any that keep to these rules, and one draw needn't show every extreme that they name: `tile_map`: row (t * 4 + c) * 3 + j is slot j of the device at tile index t and cplx index c and holds the complex, block row and block column of its tile, or -1 three times where the slot is empty. Each tile (k, r, q) with r and q below ceil(lengths[k] / 128) is held by exactly one slot and no other tile is held. Complex k is owned by cplx index k // 1; no two filled slots of one device have the same owner, and for fixed t and j the owners over the 4 cplx indices are all different.
All inputs are finite; a program needn't handle non-finite values.
Results may differ from a plain program's by a relative error of at most 0.0089.
Values sent between devices are 32-bit elements; how exact they have to be, the bound alone decides.
No kernel may reach another device: no remote copies, remote signals or barrier semaphores. Data moves between devices by JAX's collectives and lax.ppermute only.
A program may use at most 128 MiB of HBM per device.

v0:
```python
import jax
import jax.numpy as jnp
from jax import lax
from jax.sharding import PartitionSpec as P

EPS = 1e-05


def bin_centers(bin_count):
    bin_step = 31.0 / (bin_count - 2)
    return (jnp.arange(bin_count, dtype=jnp.float32) + 0.5) * bin_step


def d_zero(length):
    clipped = jnp.maximum(length, 19).astype(jnp.float32)
    return 1.24 * jnp.cbrt(clipped - 15.0) - 1.8


def pair_head(row_block, ln_gain, w_in, w_out, w_head, head_bias, centers, distance):
    values = row_block.astype(jnp.float32)
    row_mean = jnp.mean(values, axis=-1, keepdims=True)
    centred = values - row_mean
    variance = jnp.mean(centred * centred, axis=-1, keepdims=True)
    normed = (centred * lax.rsqrt(variance + EPS) * ln_gain).astype(jnp.bfloat16)
    hidden = jax.nn.relu(jnp.dot(normed, w_in, preferred_element_type=jnp.float32)).astype(
        jnp.bfloat16
    )
    updated = (values + jnp.dot(hidden, w_out, preferred_element_type=jnp.float32)).astype(
        jnp.bfloat16
    )
    logits = jnp.dot(updated, w_head, preferred_element_type=jnp.float32) + head_bias
    bin_probs = jax.nn.softmax(logits, axis=-1)
    expected = jnp.sum(bin_probs * centers, axis=-1)
    tm_term = jnp.sum(bin_probs / (1.0 + (centers / distance) ** 2), axis=-1)
    return (expected, tm_term)


def route_rows(
    error_src, rows_src, row_src, found_src, n_tile, parts_per, rows_each, tile_side, highest
):
    target_rows = jnp.arange(n_tile, dtype=jnp.int32)[:, None, None]
    part_index = jnp.arange(parts_per, dtype=jnp.int32)[None, None, :]
    routing = (
        (target_rows == row_src[None, :, None] * parts_per + part_index) & found_src[None, :, None]
    ).astype(jnp.float32)
    sender_count = error_src.shape[0]
    error_parts = error_src.reshape(sender_count, parts_per, rows_each, tile_side)
    row_parts = rows_src.reshape(sender_count, parts_per, rows_each)
    error_out = jnp.einsum("tcq,cqrj->tcrj", routing, error_parts, precision=highest)
    rows_out = jnp.einsum("tcq,cqr->tcr", routing, row_parts, precision=highest)
    return (error_out, rows_out)


def place_rows(
    error_back,
    rows_back,
    member_all,
    row_all,
    colblk_all,
    found_all,
    row_index,
    parts_per,
    cpx_dev,
    blocks,
    rows_each,
    tile_side,
    maxres,
    highest,
):
    mine_rows = found_all & (row_all == row_index // parts_per)
    member_hot = (
        (jnp.arange(cpx_dev, dtype=jnp.int32)[None, None, :] == member_all[..., None])
        & mine_rows[..., None]
    ).astype(jnp.float32)
    block_hot = (
        jnp.arange(blocks, dtype=jnp.int32)[None, None, :] == colblk_all[..., None]
    ).astype(jnp.float32)
    sources = member_all.shape[0] * member_all.shape[1]
    place_hot = (member_hot[..., :, None] * block_hot[..., None, :]).reshape(
        sources, cpx_dev, blocks
    )
    share_map = jnp.einsum(
        "smb,srj->mrbj",
        place_hot,
        error_back.reshape(sources, rows_each, tile_side),
        precision=highest,
    ).reshape(cpx_dev, rows_each, maxres)
    share_rows = jnp.einsum(
        "sm,sr->mr",
        member_hot.reshape(sources, cpx_dev),
        rows_back.reshape(sources, rows_each),
        precision=highest,
    )
    return (share_map, share_rows)


def shards(pair_tiles, tile_map, lengths, resolved, ln_gain, w_in, w_out, w_head, head_bias):
    highest = lax.Precision.HIGHEST
    n_tile = lax.axis_size("tile")
    n_cplx = lax.axis_size("cplx")
    row_index = lax.axis_index("tile")
    col_index = lax.axis_index("cplx")
    slot_count, tile_side, _, pair_width = pair_tiles.shape
    complexes, maxres = resolved.shape
    blocks = maxres // tile_side
    cpx_dev = complexes // n_cplx
    rows_each = maxres // n_tile
    parts_per = tile_side // rows_each
    centers = bin_centers(w_head.shape[1])
    positions = jnp.arange(maxres, dtype=jnp.int32)
    valid_mask = ((positions[None, :] < lengths[:, None]) & (resolved > 0)).astype(jnp.float32)
    valid_blocks = valid_mask.reshape(complexes, blocks, tile_side)
    layout = tile_map.reshape(n_tile, n_cplx, slot_count, 3)
    own_slots = layout[row_index, col_index]
    row_count = tile_side * tile_side
    block_rows = min(4096, row_count)
    error_tiles = []
    score_tiles = []
    owner_list = []
    for slot in range(slot_count):
        slot_meta = own_slots[slot]
        present = slot_meta[0] >= 0
        complex_id = jnp.maximum(slot_meta[0], 0)
        block_row = jnp.maximum(slot_meta[1], 0)
        block_col = jnp.maximum(slot_meta[2], 0)
        distance = d_zero(lengths[complex_id])

        def head_block(row_block, distance=distance):
            return pair_head(row_block, ln_gain, w_in, w_out, w_head, head_bias, centers, distance)

        expected, tm_term = lax.map(
            head_block, pair_tiles[slot].reshape(row_count // block_rows, block_rows, pair_width)
        )
        row_valid = valid_blocks[complex_id, block_row]
        col_valid = valid_blocks[complex_id, block_col]
        weight = jnp.where(present, row_valid[:, None] * col_valid[None, :], jnp.float32(0.0))
        error_tiles.append(weight * expected.reshape(tile_side, tile_side))
        score_tiles.append(weight * tm_term.reshape(tile_side, tile_side))
        owner_list.append(jnp.where(present, complex_id // cpx_dev, -1))
    owner_ids = jnp.stack(owner_list)
    select = (jnp.arange(n_cplx, dtype=jnp.int32)[:, None] == owner_ids[None, :]).astype(
        jnp.float32
    )
    error_send = jnp.einsum("os,sij->oij", select, jnp.stack(error_tiles), precision=highest)
    score_send = jnp.einsum("os,sij->oij", select, jnp.stack(score_tiles), precision=highest)
    error_in, score_in = (
        lax.all_to_all(error_send, "cplx", split_axis=0, concat_axis=0, tiled=True),
        lax.all_to_all(score_send, "cplx", split_axis=0, concat_axis=0, tiled=True),
    )
    rows_in = jnp.sum(score_in, axis=2)
    complex_all = layout[..., 0]
    owner_all = jnp.where(complex_all >= 0, complex_all // cpx_dev, -1)
    matched = owner_all == col_index
    matched_float = matched.astype(jnp.float32)
    slot_hot = matched_float[row_index]
    error_slots = jnp.einsum("sj,sab->jab", slot_hot, error_in, precision=highest)
    rows_slots = jnp.einsum("sj,sa->ja", slot_hot, rows_in, precision=highest)
    found_slot = jnp.any(matched, axis=1)

    def pick_slot(column):
        return jnp.sum(jnp.where(matched, layout[..., column], 0), axis=1)

    member_slot = pick_slot(0) - col_index * cpx_dev
    row_slot = pick_slot(1)
    colblk_slot = pick_slot(2)
    error_out, rows_out = route_rows(
        error_slots,
        rows_slots,
        row_slot[row_index],
        found_slot[row_index],
        n_tile,
        parts_per,
        rows_each,
        tile_side,
        highest,
    )
    error_back, rows_back = (
        lax.all_to_all(error_out, "tile", split_axis=0, concat_axis=0, tiled=True),
        lax.all_to_all(rows_out, "tile", split_axis=0, concat_axis=0, tiled=True),
    )
    share_map, share_rows = place_rows(
        error_back,
        rows_back,
        member_slot,
        row_slot,
        colblk_slot,
        found_slot,
        row_index,
        parts_per,
        cpx_dev,
        blocks,
        rows_each,
        tile_side,
        maxres,
        highest,
    )
    valid_rows = lax.dynamic_slice(
        valid_mask, (col_index * cpx_dev, row_index * rows_each), (cpx_dev, rows_each)
    )
    totals = lax.dynamic_slice_in_dim(jnp.sum(valid_mask, axis=1), col_index * cpx_dev, cpx_dev)
    denominator = jnp.maximum(valid_rows * totals[:, None], jnp.float32(1.0))
    residue_error = jnp.sum(share_map, axis=2) / denominator
    best_share = jnp.max(share_rows / denominator, axis=1)
    tm_score = lax.pmax(best_share, "tile")
    return (share_map, residue_error, tm_score)


def solution(mesh):
    placed = (P(("tile", "cplx"), None, None, None), P(), P(), P(), P(), P(), P(), P(), P())
    return jax.shard_map(
        shards,
        mesh=mesh,
        in_specs=placed,
        out_specs=(P("cplx", "tile", None), P("cplx", "tile"), P("cplx")),
        check_vma=False,
    )
```

profile of v0, /device:TPU:0, one launch (start us, length us, event | category | flops | bytes accessed | tf_op | source)
XLA Modules:
  0.0 221.4 jit_solution(597201668748234575)
XLA Ops:
  6.2 8.9 %fusion.147 = (bf16[1,128,128,128]{3,2,1,0:T(8,128)(2,1)}, bf16[1,128,128,128]{3,2,1,0:T(8,128)(2,1)}, bf16[1,128,128,128]{3,2,1,0:T(8,128)(2,1)}) fusion(bf16[3,128,128,128]{3,2,1,0:T(8,128)(2,1)} %param.15), kind=kLoop, calls=%fused_computation.187 | loop fusion | bytes 25165824 | tf_op jit(solution)/shard_map/slice | solution.py:132
  16.5 38.7 %while.44 = (s32[]{:T(128)}, f32[4,4096]{1,0:T(4,128)S(1)}, f32[4,4096]{1,0:T(4,128)S(1)}, bf16[4,4096,128]{2,1,0:T(8,128)(2,1)}, f32[128]{0:T(128)S(1)}, /*inde...) while((s32[]{:T(128)}, f32[4,4096]{1,0:T(4,128)S(1)}, ...), condition=%wide.region_23.24_spmd.clone.clone, body=%wide.region_16.23_spmd.clone.clone.sunk | while | flops 1155256576 | bytes 10046353 | solution.py:131
  16.5 1.6 convert_reduce_fusion.8
  18.1 2.3 %fusion.225 = f32[4096]{0:T(1024)S(1)} fusion(f32[4096]{0:T(1024)S(1)} %broadcast_multiply_fusion.8, bf16[4,4096,128]{2,1,0:T(8,128)(2,1)} %get-tuple-element.704, s32[]{:T(128)S(6)} %copy.88), kind=kLoop, calls=%fused_computation.68.clone.1 | loop fusion | flops 2093056 | bytes 1081348 | tf_op jit(solution)/shard_map/while/body/eval_jaxpr/reduce_sum | solution.py:23
  20.4 4.1 %fusion.226 = bf16[4096,128]{1,0:T(8,128)(2,1)S(1)} fusion(bf16[512,128]{1,0:T(8,128)(2,1)S(1)} %get-tuple-element.707, bf16[128,512]{1,0:T(8,128)(2,1)S(1)} %get-tuple-element.706, f32[128]{0:T(128)S(1)} %get-tuple-element.705, f32[4096]{0:T(1024)S(1)} %add_rsqrt_fusion.8, f32[4096]{0:T(1024)S(1)} %broadcast_multiply_fusion.8, ...), kind=kOutput, calls=%fused_computation.61.clone.1 | convolution fusion | flops 1082130432 | bytes 3442176 | tf_op jit(solution)/shard_map/while/body/eval_jaxpr/dot_general | solution.py:28
  26.3 1.6 convert_reduce_fusion.8
  27.8 2.3 %fusion.225 = f32[4096]{0:T(1024)S(1)} fusion(f32[4096]{0:T(1024)S(1)} %broadcast_multiply_fusion.8, bf16[4,4096,128]{2,1,0:T(8,128)(2,1)} %get-tuple-element.704, s32[]{:T(128)S(6)} %copy.88), kind=kLoop, calls=%fused_computation.68.clone.1 | loop fusion | flops 2093056 | bytes 1081348 | tf_op jit(solution)/shard_map/while/body/eval_jaxpr/reduce_sum | solution.py:23
  30.2 4.0 %fusion.226 = bf16[4096,128]{1,0:T(8,128)(2,1)S(1)} fusion(bf16[512,128]{1,0:T(8,128)(2,1)S(1)} %get-tuple-element.707, bf16[128,512]{1,0:T(8,128)(2,1)S(1)} %get-tuple-element.706, f32[128]{0:T(128)S(1)} %get-tuple-element.705, f32[4096]{0:T(1024)S(1)} %add_rsqrt_fusion.8, f32[4096]{0:T(1024)S(1)} %broadcast_multiply_fusion.8, ...), kind=kOutput, calls=%fused_computation.61.clone.1 | convolution fusion | flops 1082130432 | bytes 3442176 | tf_op jit(solution)/shard_map/while/body/eval_jaxpr/dot_general | solution.py:28
  35.9 1.6 convert_reduce_fusion.8
  37.5 2.3 %fusion.225 = f32[4096]{0:T(1024)S(1)} fusion(f32[4096]{0:T(1024)S(1)} %broadcast_multiply_fusion.8, bf16[4,4096,128]{2,1,0:T(8,128)(2,1)} %get-tuple-element.704, s32[]{:T(128)S(6)} %copy.88), kind=kLoop, calls=%fused_computation.68.clone.1 | loop fusion | flops 2093056 | bytes 1081348 | tf_op jit(solution)/shard_map/while/body/eval_jaxpr/reduce_sum | solution.py:23
  39.8 4.2 %fusion.226 = bf16[4096,128]{1,0:T(8,128)(2,1)S(1)} fusion(bf16[512,128]{1,0:T(8,128)(2,1)S(1)} %get-tuple-element.707, bf16[128,512]{1,0:T(8,128)(2,1)S(1)} %get-tuple-element.706, f32[128]{0:T(128)S(1)} %get-tuple-element.705, f32[4096]{0:T(1024)S(1)} %add_rsqrt_fusion.8, f32[4096]{0:T(1024)S(1)} %broadcast_multiply_fusion.8, ...), kind=kOutput, calls=%fused_computation.61.clone.1 | convolution fusion | flops 1082130432 | bytes 3442176 | tf_op jit(solution)/shard_map/while/body/eval_jaxpr/dot_general | solution.py:28
  45.6 1.6 convert_reduce_fusion.8
  47.2 2.3 %fusion.225 = f32[4096]{0:T(1024)S(1)} fusion(f32[4096]{0:T(1024)S(1)} %broadcast_multiply_fusion.8, bf16[4,4096,128]{2,1,0:T(8,128)(2,1)} %get-tuple-element.704, s32[]{:T(128)S(6)} %copy.88), kind=kLoop, calls=%fused_computation.68.clone.1 | loop fusion | flops 2093056 | bytes 1081348 | tf_op jit(solution)/shard_map/while/body/eval_jaxpr/reduce_sum | solution.py:23
  49.6 4.0 %fusion.226 = bf16[4096,128]{1,0:T(8,128)(2,1)S(1)} fusion(bf16[512,128]{1,0:T(8,128)(2,1)S(1)} %get-tuple-element.707, bf16[128,512]{1,0:T(8,128)(2,1)S(1)} %get-tuple-element.706, f32[128]{0:T(128)S(1)} %get-tuple-element.705, f32[4096]{0:T(1024)S(1)} %add_rsqrt_fusion.8, f32[4096]{0:T(1024)S(1)} %broadcast_multiply_fusion.8, ...), kind=kOutput, calls=%fused_computation.61.clone.1 | convolution fusion | flops 1082130432 | bytes 3442176 | tf_op jit(solution)/shard_map/while/body/eval_jaxpr/dot_general | solution.py:28
  60.1 39.0 %while.42 = (s32[]{:T(128)}, f32[4,4096]{1,0:T(4,128)S(1)}, f32[4,4096]{1,0:T(4,128)S(1)}, bf16[4,4096,128]{2,1,0:T(8,128)(2,1)}, f32[128]{0:T(128)S(1)}, /*inde...) while((s32[]{:T(128)}, f32[4,4096]{1,0:T(4,128)S(1)}, ...), condition=%wide.region_7.8_spmd.clone.clone, body=%wide.region_0.7_spmd.clone.clone.sunk | while | flops 1155256576 | bytes 10046353 | solution.py:131
  60.1 1.6 convert_reduce_fusion.6
  61.7 2.3 %fusion.203 = f32[4096]{0:T(1024)S(1)} fusion(f32[4096]{0:T(1024)S(1)} %broadcast_multiply_fusion.6, bf16[4,4096,128]{2,1,0:T(8,128)(2,1)} %get-tuple-element.740, s32[]{:T(128)S(6)} %copy.97), kind=kLoop, calls=%fused_computation.12.clone.1 | loop fusion | flops 2093056 | bytes 1081348 | tf_op jit(solution)/shard_map/while/body/eval_jaxpr/reduce_sum | solution.py:23
  64.0 4.1 %fusion.204 = bf16[4096,128]{1,0:T(8,128)(2,1)S(1)} fusion(bf16[512,128]{1,0:T(8,128)(2,1)S(1)} %get-tuple-element.743, bf16[128,512]{1,0:T(8,128)(2,1)S(1)} %get-tuple-element.742, f32[128]{0:T(128)S(1)} %get-tuple-element.741, f32[4096]{0:T(1024)S(1)} %add_rsqrt_fusion.6, f32[4096]{0:T(1024)S(1)} %broadcast_multiply_fusion.6, ...), kind=kOutput, calls=%fused_computation.5.clone.1 | convolution fusion | flops 1082130432 | bytes 3442176 | tf_op jit(solution)/shard_map/while/body/eval_jaxpr/dot_general | solution.py:28
  69.8 1.6 convert_reduce_fusion.6
  71.4 2.3 %fusion.203 = f32[4096]{0:T(1024)S(1)} fusion(f32[4096]{0:T(1024)S(1)} %broadcast_multiply_fusion.6, bf16[4,4096,128]{2,1,0:T(8,128)(2,1)} %get-tuple-element.740, s32[]{:T(128)S(6)} %copy.97), kind=kLoop, calls=%fused_computation.12.clone.1 | loop fusion | flops 2093056 | bytes 1081348 | tf_op jit(solution)/shard_map/while/body/eval_jaxpr/reduce_sum | solution.py:23
  73.7 4.1 %fusion.204 = bf16[4096,128]{1,0:T(8,128)(2,1)S(1)} fusion(bf16[512,128]{1,0:T(8,128)(2,1)S(1)} %get-tuple-element.743, bf16[128,512]{1,0:T(8,128)(2,1)S(1)} %get-tuple-element.742, f32[128]{0:T(128)S(1)} %get-tuple-element.741, f32[4096]{0:T(1024)S(1)} %add_rsqrt_fusion.6, f32[4096]{0:T(1024)S(1)} %broadcast_multiply_fusion.6, ...), kind=kOutput, calls=%fused_computation.5.clone.1 | convolution fusion | flops 1082130432 | bytes 3442176 | tf_op jit(solution)/shard_map/while/body/eval_jaxpr/dot_general | solution.py:28
  79.5 1.6 convert_reduce_fusion.6
  81.1 2.3 %fusion.203 = f32[4096]{0:T(1024)S(1)} fusion(f32[4096]{0:T(1024)S(1)} %broadcast_multiply_fusion.6, bf16[4,4096,128]{2,1,0:T(8,128)(2,1)} %get-tuple-element.740, s32[]{:T(128)S(6)} %copy.97), kind=kLoop, calls=%fused_computation.12.clone.1 | loop fusion | flops 2093056 | bytes 1081348 | tf_op jit(solution)/shard_map/while/body/eval_jaxpr/reduce_sum | solution.py:23
  83.4 4.2 %fusion.204 = bf16[4096,128]{1,0:T(8,128)(2,1)S(1)} fusion(bf16[512,128]{1,0:T(8,128)(2,1)S(1)} %get-tuple-element.743, bf16[128,512]{1,0:T(8,128)(2,1)S(1)} %get-tuple-element.742, f32[128]{0:T(128)S(1)} %get-tuple-element.741, f32[4096]{0:T(1024)S(1)} %add_rsqrt_fusion.6, f32[4096]{0:T(1024)S(1)} %broadcast_multiply_fusion.6, ...), kind=kOutput, calls=%fused_computation.5.clone.1 | convolution fusion | flops 1082130432 | bytes 3442176 | tf_op jit(solution)/shard_map/while/body/eval_jaxpr/dot_general | solution.py:28
  89.2 1.6 convert_reduce_fusion.6
  90.8 2.3 %fusion.203 = f32[4096]{0:T(1024)S(1)} fusion(f32[4096]{0:T(1024)S(1)} %broadcast_multiply_fusion.6, bf16[4,4096,128]{2,1,0:T(8,128)(2,1)} %get-tuple-element.740, s32[]{:T(128)S(6)} %copy.97), kind=kLoop, calls=%fused_computation.12.clone.1 | loop fusion | flops 2093056 | bytes 1081348 | tf_op jit(solution)/shard_map/while/body/eval_jaxpr/reduce_sum | solution.py:23
  93.2 4.2 %fusion.204 = bf16[4096,128]{1,0:T(8,128)(2,1)S(1)} fusion(bf16[512,128]{1,0:T(8,128)(2,1)S(1)} %get-tuple-element.743, bf16[128,512]{1,0:T(8,128)(2,1)S(1)} %get-tuple-element.742, f32[128]{0:T(128)S(1)} %get-tuple-element.741, f32[4096]{0:T(1024)S(1)} %add_rsqrt_fusion.6, f32[4096]{0:T(1024)S(1)} %broadcast_multiply_fusion.6, ...), kind=kOutput, calls=%fused_computation.5.clone.1 | convolution fusion | flops 1082130432 | bytes 3442176 | tf_op jit(solution)/shard_map/while/body/eval_jaxpr/dot_general | solution.py:28
  100.0 38.7 %while.43 = (s32[]{:T(128)}, f32[4,4096]{1,0:T(4,128)S(1)}, f32[4,4096]{1,0:T(4,128)S(1)}, bf16[4,4096,128]{2,1,0:T(8,128)(2,1)}, f32[128]{0:T(128)S(1)}, /*inde...) while((s32[]{:T(128)}, f32[4,4096]{1,0:T(4,128)S(1)}, ...), condition=%wide.region_15.16_spmd.clone.clone, body=%wide.region_8.15_spmd.clone.clone.sunk | while | flops 1155256576 | bytes 10046353 | solution.py:131
  100.0 1.6 convert_reduce_fusion.7
  101.6 2.3 %fusion.214 = f32[4096]{0:T(1024)S(1)} fusion(f32[4096]{0:T(1024)S(1)} %broadcast_multiply_fusion.7, bf16[4,4096,128]{2,1,0:T(8,128)(2,1)} %get-tuple-element.776, s32[]{:T(128)S(6)} %copy.106), kind=kLoop, calls=%fused_computation.40.clone.1 | loop fusion | flops 2093056 | bytes 1081348 | tf_op jit(solution)/shard_map/while/body/eval_jaxpr/reduce_sum | solution.py:23
  103.9 4.0 %fusion.215 = bf16[4096,128]{1,0:T(8,128)(2,1)S(1)} fusion(bf16[512,128]{1,0:T(8,128)(2,1)S(1)} %get-tuple-element.779, bf16[128,512]{1,0:T(8,128)(2,1)S(1)} %get-tuple-element.778, f32[128]{0:T(128)S(1)} %get-tuple-element.777, f32[4096]{0:T(1024)S(1)} %add_rsqrt_fusion.7, f32[4096]{0:T(1024)S(1)} %broadcast_multiply_fusion.7, ...), kind=kOutput, calls=%fused_computation.33.clone.1 | convolution fusion | flops 1082130432 | bytes 3442176 | tf_op jit(solution)/shard_map/while/body/eval_jaxpr/dot_general | solution.py:28
  109.6 1.6 convert_reduce_fusion.7
  111.2 2.3 %fusion.214 = f32[4096]{0:T(1024)S(1)} fusion(f32[4096]{0:T(1024)S(1)} %broadcast_multiply_fusion.7, bf16[4,4096,128]{2,1,0:T(8,128)(2,1)} %get-tuple-element.776, s32[]{:T(128)S(6)} %copy.106), kind=kLoop, calls=%fused_computation.40.clone.1 | loop fusion | flops 2093056 | bytes 1081348 | tf_op jit(solution)/shard_map/while/body/eval_jaxpr/reduce_sum | solution.py:23
  113.5 4.0 %fusion.215 = bf16[4096,128]{1,0:T(8,128)(2,1)S(1)} fusion(bf16[512,128]{1,0:T(8,128)(2,1)S(1)} %get-tuple-element.779, bf16[128,512]{1,0:T(8,128)(2,1)S(1)} %get-tuple-element.778, f32[128]{0:T(128)S(1)} %get-tuple-element.777, f32[4096]{0:T(1024)S(1)} %add_rsqrt_fusion.7, f32[4096]{0:T(1024)S(1)} %broadcast_multiply_fusion.7, ...), kind=kOutput, calls=%fused_computation.33.clone.1 | convolution fusion | flops 1082130432 | bytes 3442176 | tf_op jit(solution)/shard_map/while/body/eval_jaxpr/dot_general | solution.py:28
  119.2 1.6 convert_reduce_fusion.7
  120.8 2.3 %fusion.214 = f32[4096]{0:T(1024)S(1)} fusion(f32[4096]{0:T(1024)S(1)} %broadcast_multiply_fusion.7, bf16[4,4096,128]{2,1,0:T(8,128)(2,1)} %get-tuple-element.776, s32[]{:T(128)S(6)} %copy.106), kind=kLoop, calls=%fused_computation.40.clone.1 | loop fusion | flops 2093056 | bytes 1081348 | tf_op jit(solution)/shard_map/while/body/eval_jaxpr/reduce_sum | solution.py:23
  123.2 4.0 %fusion.215 = bf16[4096,128]{1,0:T(8,128)(2,1)S(1)} fusion(bf16[512,128]{1,0:T(8,128)(2,1)S(1)} %get-tuple-element.779, bf16[128,512]{1,0:T(8,128)(2,1)S(1)} %get-tuple-element.778, f32[128]{0:T(128)S(1)} %get-tuple-element.777, f32[4096]{0:T(1024)S(1)} %add_rsqrt_fusion.7, f32[4096]{0:T(1024)S(1)} %broadcast_multiply_fusion.7, ...), kind=kOutput, calls=%fused_computation.33.clone.1 | convolution fusion | flops 1082130432 | bytes 3442176 | tf_op jit(solution)/shard_map/while/body/eval_jaxpr/dot_general | solution.py:28
  130.4 2.3 %fusion.214 = f32[4096]{0:T(1024)S(1)} fusion(f32[4096]{0:T(1024)S(1)} %broadcast_multiply_fusion.7, bf16[4,4096,128]{2,1,0:T(8,128)(2,1)} %get-tuple-element.776, s32[]{:T(128)S(6)} %copy.106), kind=kLoop, calls=%fused_computation.40.clone.1 | loop fusion | flops 2093056 | bytes 1081348 | tf_op jit(solution)/shard_map/while/body/eval_jaxpr/reduce_sum | solution.py:23
  132.7 4.1 %fusion.215 = bf16[4096,128]{1,0:T(8,128)(2,1)S(1)} fusion(bf16[512,128]{1,0:T(8,128)(2,1)S(1)} %get-tuple-element.779, bf16[128,512]{1,0:T(8,128)(2,1)S(1)} %get-tuple-element.778, f32[128]{0:T(128)S(1)} %get-tuple-element.777, f32[4096]{0:T(1024)S(1)} %add_rsqrt_fusion.7, f32[4096]{0:T(1024)S(1)} %broadcast_multiply_fusion.7, ...), kind=kOutput, calls=%fused_computation.33.clone.1 | convolution fusion | flops 1082130432 | bytes 3442176 | tf_op jit(solution)/shard_map/while/body/eval_jaxpr/dot_general | solution.py:28
  140.8 4.2 %all-to-all-start = ((f32[4,128,128]{2,1,0:T(8,128)}), f32[4,128,128]{2,1,0:T(8,128)S(1)}, u32[]{:S(2)}, u32[]{:S(2)}) async-start(f32[4,128,128]{2,1,0:T(8,128)} %copy.42), calls=%async_computation | async-start | bytes 524288 | tf_op jit(solution)/shard_map/all_to_all | solution.py:147
  147.4 3.6 %all-to-all-done = f32[4,128,128]{2,1,0:T(8,128)S(1)} async-done(((f32[4,128,128]{2,1,0:T(8,128)}), f32[4,128,128]{2,1,0:T(8,128)S(1)}, u32[]{:S(2)}, u32[]{:S(2)}) %all-to-all-start) | async-done | bytes 262176 | tf_op jit(solution)/shard_map/all_to_all | solution.py:147
  151.1 3.4 %all-to-all-start.2 = ((f32[4,128,128]{2,1,0:T(8,128)}), f32[4,128,128]{2,1,0:T(8,128)S(1)}, u32[]{:S(2)}, u32[]{:S(2)}) async-start(f32[4,128,128]{2,1,0:T(8,128)} %copy.52), calls=%async_computation.2 | async-start | bytes 524288 | tf_op jit(solution)/shard_map/all_to_all | solution.py:148
  155.0 5.4 %all-to-all-done.2 = f32[4,128,128]{2,1,0:T(8,128)S(1)} async-done(((f32[4,128,128]{2,1,0:T(8,128)}), f32[4,128,128]{2,1,0:T(8,128)S(1)}, u32[]{:S(2)}, u32[]{:S(2)}) %all-to-all-start.2) | async-done | bytes 262176 | tf_op jit(solution)/shard_map/all_to_all | solution.py:148
  161.9 6.4 %all-to-all-start.3 = ((f32[8,1,192]{2,1,0:T(1,128)}), f32[8,1,192]{2,1,0:T(1,128)S(1)}, u32[]{:S(2)}, u32[]{:S(2)}) async-start(f32[8,1,192]{2,1,0:T(1,128)} %reshape.699), calls=%async_computation.3 | async-start | bytes 16384 | tf_op jit(solution)/shard_map/all_to_all | solution.py:179
  170.0 4.9 %all-to-all-done.3 = f32[8,1,192]{2,1,0:T(1,128)S(1)} async-done(((f32[8,1,192]{2,1,0:T(1,128)}), f32[8,1,192]{2,1,0:T(1,128)S(1)}, u32[]{:S(2)}, u32[]{:S(2)}) %all-to-all-start.3) | async-done | bytes 6176 | tf_op jit(solution)/shard_map/all_to_all | solution.py:179
  174.9 3.5 %all-to-all-start.1 = ((f32[8,3,64,128]{3,2,1,0:T(8,128)}), f32[8,3,64,128]{3,2,1,0:T(8,128)S(1)}, u32[]{:S(2)}, u32[]{:S(2)}) async-start(f32[8,3,64,128]{3,2,1,0:T(8,128)} %copy.47), calls=%async_computation.1 | async-start | bytes 1572864 | tf_op jit(solution)/shard_map/all_to_all | solution.py:178
  180.6 16.5 %all-to-all-done.1 = f32[8,3,64,128]{3,2,1,0:T(8,128)S(1)} async-done(((f32[8,3,64,128]{3,2,1,0:T(8,128)}), f32[8,3,64,128]{3,2,1,0:T(8,128)S(1)}, u32[]{:S(2)}, u32[]{:S(2)}) %all-to-all-start.1) | async-done | bytes 786464 | tf_op jit(solution)/shard_map/all_to_all | solution.py:178
  201.4 20.0 %pmax.7 = f32[1]{0:T(128)} all-reduce(f32[1]{0:T(128)} %bitcast.53), channel_id=1, replica_groups=mesh['tile'=8,'cplx'=4] {'tile'}, use_global_device_ids=true, to_apply=%region_32.33 | all-reduce | flops 1 | bytes 8 | tf_op jit(solution)/shard_map/pmax | solution.py:204
  (171 shorter events, 38.2 us)
Async XLA Ops:
  6.1 9.0 %copy-start.3 = (s32[4]{0:T(128)S(1)}, s32[4]{0:T(128)}, u32[]{:S(2)}) copy-start(s32[4]{0:T(128)} %param.17) | copy-start | bytes 52
  6.1 10.3 %copy-start = (bf16[128,64]{0,1:T(8,128)(2,1)S(1)}, bf16[128,64]{0,1:T(8,128)(2,1)}, u32[]{:S(2)}) copy-start(bf16[128,64]{0,1:T(8,128)(2,1)} %param.22) | copy-start | bytes 49156
  6.2 10.3 %copy-start.1 = (f32[64]{0:T(128)S(1)}, f32[64]{0:T(128)}, u32[]{:S(2)}) copy-start(f32[64]{0:T(128)} %param.23) | copy-start | bytes 772
  6.2 10.3 %copy-start.4 = (bf16[128,512]{1,0:T(8,128)(2,1)S(1)}, bf16[128,512]{1,0:T(8,128)(2,1)}, u32[]{:S(2)}) copy-start(bf16[128,512]{1,0:T(8,128)(2,1)} %param.20) | copy-start | bytes 393220
  6.2 10.3 %copy-start.5 = (bf16[512,128]{1,0:T(8,128)(2,1)S(1)}, bf16[512,128]{1,0:T(8,128)(2,1)}, u32[]{:S(2)}) copy-start(bf16[512,128]{1,0:T(8,128)(2,1)} %param.21) | copy-start | bytes 393220
  6.2 10.3 %copy-start.6 = (f32[128]{0:T(128)S(1)}, f32[128]{0:T(128)}, u32[]{:S(2)}) copy-start(f32[128]{0:T(128)} %param.19) | copy-start | bytes 1540
  16.5 38.8 %copy-start.2 = (s32[4,512]{1,0:T(4,128)S(1)}, s32[4,512]{1,0:T(4,128)}, u32[]{:S(2)}) copy-start(s32[4,512]{1,0:T(4,128)} %param.18) | copy-start | bytes 24580
  140.8 10.2 %all-to-all-start = ((f32[4,128,128]{2,1,0:T(8,128)}), f32[4,128,128]{2,1,0:T(8,128)S(1)}, u32[]{:S(2)}, u32[]{:S(2)}) async-start(f32[4,128,128]{2,1,0:T(8,128)} %copy.42), calls=%async_computation | async-start | bytes 524288 | tf_op jit(solution)/shard_map/all_to_all | solution.py:147
  151.1 9.4 %all-to-all-start.2 = ((f32[4,128,128]{2,1,0:T(8,128)}), f32[4,128,128]{2,1,0:T(8,128)S(1)}, u32[]{:S(2)}, u32[]{:S(2)}) async-start(f32[4,128,128]{2,1,0:T(8,128)} %copy.52), calls=%async_computation.2 | async-start | bytes 524288 | tf_op jit(solution)/shard_map/all_to_all | solution.py:148
  161.9 13.0 %all-to-all-start.3 = ((f32[8,1,192]{2,1,0:T(1,128)}), f32[8,1,192]{2,1,0:T(1,128)S(1)}, u32[]{:S(2)}, u32[]{:S(2)}) async-start(f32[8,1,192]{2,1,0:T(1,128)} %reshape.699), calls=%async_computation.3 | async-start | bytes 16384 | tf_op jit(solution)/shard_map/all_to_all | solution.py:179
  174.9 22.3 %all-to-all-start.1 = ((f32[8,3,64,128]{3,2,1,0:T(8,128)}), f32[8,3,64,128]{3,2,1,0:T(8,128)S(1)}, u32[]{:S(2)}, u32[]{:S(2)}) async-start(f32[8,3,64,128]{3,2,1,0:T(8,128)} %copy.47), calls=%async_computation.1 | async-start | bytes 1572864 | tf_op jit(solution)/shard_map/all_to_all | solution.py:178
where the time goes:
time: 223 us; the launch traced here: 221 us
  matrix products  59.7 us (27%)
  other arithmetic  57.5 us (26%)
  waiting for transfers between devices  30.4 us (14%)
  local copies, waits for them, and re-layouts  24.1 us (11%)
  blocking collectives  20 us (9%)
  starting transfers between devices  17.6 us (8%)
  between operations  10.8 us (5%)
    dot_general x12, matrix products, pair_head(): jnp.dot(hidden, w_out, preferred_element_type=jnp.float32)  48.9 us
    reduce_sum x12, other arithmetic, pair_head(): variance = jnp.mean(centred * centred, axis=-1, keepdims=True)  27.9 us
    pmax x1, blocking collectives, shards(): tm_score = lax.pmax(best_share, 'tile')  20 us
    reduce_sum x12, other arithmetic, pair_head(): row_mean = jnp.mean(values, axis=-1, keepdims=True)  18.9 us
    all_to_all x1, waiting for transfers between devices, shards(): lax.all_to_all(error_out, 'tile', split_axis=0, concat_axis=0, tiled=True)  16.5 us
    slice x1, local copies, waits for them, and re-layouts, shards(): pair_tiles[slot].reshape(row_count // block_rows, block_rows, pair_width)  8.89 us
    all_to_all x1, starting transfers between devices, shards(): lax.all_to_all(rows_out, 'tile', split_axis=0, concat_axis=0, tiled=True)  6.45 us
    dynamic_update_slice x24, local copies, waits for them, and re-layouts, shards(): lax.map(head_block, pair_tiles[slot].reshape(row_count // block_rows, blo...  5.96 us
  transfers between devices with their start and end apart: 4, of which 4 were waited for; matrix products, arithmetic and copies ran while one was open for 3% of the time, Pallas kernels for 0%

commit v1 on v0

--- a/solution.py
+++ b/solution.py
@@ -174,9 +174,25 @@
         tile_side,
         highest,
     )
+
+    def view_waves(shard_in, lane_axis):
+        after, t1 = (lax.axis_size(lane_axis), lax.axis_index(lane_axis))
+        far_arr = shard_in.shape[0] // after
+        value_now = list(shard_in.shape)
+        value_now[0] = far_arr
+        x_next = value_now[0]
+        value_now[0] = x_next * after
+        k_now = jnp.zeros(value_now, shard_in.dtype)
+        for s in range(after):
+            kept_arr = lax.dynamic_slice_in_dim(shard_in, (t1 ^ s) * far_arr, far_arr, axis=0)
+            if s:
+                kept_arr = lax.ppermute(kept_arr, lane_axis, [(at, at ^ s) for at in range(after)])
+            k_now = lax.dynamic_update_slice_in_dim(k_now, kept_arr, (t1 ^ s) * x_next, axis=0)
+        return k_now
+
     error_back, rows_back = (
         lax.all_to_all(error_out, "tile", split_axis=0, concat_axis=0, tiled=True),
-        lax.all_to_all(rows_out, "tile", split_axis=0, concat_axis=0, tiled=True),
+        view_waves(rows_out, "tile"),
     )
     share_map, share_rows = place_rows(
         error_back,

time: 223 us -> 214 us (0.960)
  waiting for transfers between devices: 30.4 us -> 10.9 us
  starting transfers between devices: 17.6 us -> 29.5 us
    all_to_all x1, waiting for transfers between devices: 16.5 us -> 0.01 us  [shards(): lax.all_to_all(error_out, 'tile', split_axis=0, concat_axis=0, tiled=True)]
    ppermute x0 -> x7, starting transfers between devices: none -> 15.4 us  [view_waves(): lax.ppermute(kept_arr, lane_axis, [(at, at ^ s) for at in range(after)])]
    all_to_all x1 -> x0, starting transfers between devices: 6.45 us -> none  [shards(): lax.all_to_all(rows_out, 'tile', split_axis=0, concat_axis=0, tiled=True)]
    all_to_all x1 -> x0, waiting for transfers between devices: 4.86 us -> none  [shards(): lax.all_to_all(rows_out, 'tile', split_axis=0, concat_axis=0, tiled=True)]
    ppermute x0 -> x7, waiting for transfers between devices: none -> 3.44 us  [view_waves(): lax.ppermute(kept_arr, lane_axis, [(at, at ^ s) for at in range(after)])]
    all_to_all x1, starting transfers between devices: 3.55 us -> 6.45 us  [shards(): lax.all_to_all(error_out, 'tile', split_axis=0, concat_axis=0, tiled=True)]
  transfers between devices with their start and end apart: 4 -> 10, of which waited for: 4 -> 4; matrix products, arithmetic and copies ran while one was open for 3% -> 3% of each run, Pallas kernels for 0% -> 0%
where the time goes in v1:
time: 214 us; the launch traced here: 212 us
  matrix products  59.7 us (28%)
  other arithmetic  56.8 us (27%)
  starting transfers between devices  29.5 us (14%)
  local copies, waits for them, and re-layouts  23.2 us (11%)
  blocking collectives  20.2 us (9%)
  waiting for transfers between devices  10.9 us (5%)
  between operations  10.8 us (5%)
    dot_general x12, matrix products, pair_head(): jnp.dot(hidden, w_out, preferred_element_type=jnp.float32)  48.9 us
    reduce_sum x12, other arithmetic, pair_head(): variance = jnp.mean(centred * centred, axis=-1, keepdims=True)  27.9 us
    pmax x1, blocking collectives, shards(): tm_score = lax.pmax(best_share, 'tile')  20.2 us
    reduce_sum x12, other arithmetic, pair_head(): row_mean = jnp.mean(values, axis=-1, keepdims=True)  18.9 us
    ppermute x7, starting transfers between devices, view_waves(): lax.ppermute(kept_arr, lane_axis, [(at, at ^ s) for at in range(after)])  15.4 us
    slice x1, local copies, waits for them, and re-layouts, shards(): pair_tiles[slot].reshape(row_count // block_rows, block_rows, pair_width)  8.89 us
    all_to_all x1, starting transfers between devices, shards(): lax.all_to_all(error_out, 'tile', split_axis=0, concat_axis=0, tiled=True)  6.45 us
    dynamic_update_slice x24, local copies, waits for them, and re-layouts, shards(): lax.map(head_block, pair_tiles[slot].reshape(row_count // block_rows, blo...  5.96 us
  transfers between devices with their start and end apart: 10, of which 4 were waited for; matrix products, arithmetic and copies ran while one was open for 3% of the time, Pallas kernels for 0%

profile of v1, /device:TPU:0, one launch (start us, length us, event | category | flops | bytes accessed | tf_op | source)
XLA Modules:
  0.0 212.4 jit_solution(5217784567056216195)
XLA Ops:
  6.2 8.9 %fusion.155 = (bf16[1,128,128,128]{3,2,1,0:T(8,128)(2,1)}, bf16[1,128,128,128]{3,2,1,0:T(8,128)(2,1)}, bf16[1,128,128,128]{3,2,1,0:T(8,128)(2,1)}) fusion(bf16[3,128,128,128]{3,2,1,0:T(8,128)(2,1)} %param.15), kind=kLoop, calls=%fused_computation.202 | loop fusion | bytes 25165824 | tf_op jit(solution)/shard_map/slice | solution.py:132
  16.5 38.7 %while.44 = (s32[]{:T(128)}, f32[4,4096]{1,0:T(4,128)S(1)}, f32[4,4096]{1,0:T(4,128)S(1)}, bf16[4,4096,128]{2,1,0:T(8,128)(2,1)}, f32[128]{0:T(128)S(1)}, /*inde...) while((s32[]{:T(128)}, f32[4,4096]{1,0:T(4,128)S(1)}, ...), condition=%wide.region_23.24_spmd.clone.clone, body=%wide.region_16.23_spmd.clone.clone.sunk | while | flops 1155256576 | bytes 10046353 | solution.py:131
  16.5 1.6 convert_reduce_fusion.8
  18.1 2.3 %fusion.234 = f32[4096]{0:T(1024)S(1)} fusion(f32[4096]{0:T(1024)S(1)} %broadcast_multiply_fusion.8, bf16[4,4096,128]{2,1,0:T(8,128)(2,1)} %get-tuple-element.712, s32[]{:T(128)S(6)} %copy.83), kind=kLoop, calls=%fused_computation.68.clone.1 | loop fusion | flops 2093056 | bytes 1081348 | tf_op jit(solution)/shard_map/while/body/eval_jaxpr/reduce_sum | solution.py:23
  20.4 4.1 %fusion.235 = bf16[4096,128]{1,0:T(8,128)(2,1)S(1)} fusion(bf16[512,128]{1,0:T(8,128)(2,1)S(1)} %get-tuple-element.715, bf16[128,512]{1,0:T(8,128)(2,1)S(1)} %get-tuple-element.714, f32[128]{0:T(128)S(1)} %get-tuple-element.713, f32[4096]{0:T(1024)S(1)} %add_rsqrt_fusion.8, f32[4096]{0:T(1024)S(1)} %broadcast_multiply_fusion.8, ...), kind=kOutput, calls=%fused_computation.61.clone.1 | convolution fusion | flops 1082130432 | bytes 3442176 | tf_op jit(solution)/shard_map/while/body/eval_jaxpr/dot_general | solution.py:28
  26.3 1.6 convert_reduce_fusion.8
  27.8 2.3 %fusion.234 = f32[4096]{0:T(1024)S(1)} fusion(f32[4096]{0:T(1024)S(1)} %broadcast_multiply_fusion.8, bf16[4,4096,128]{2,1,0:T(8,128)(2,1)} %get-tuple-element.712, s32[]{:T(128)S(6)} %copy.83), kind=kLoop, calls=%fused_computation.68.clone.1 | loop fusion | flops 2093056 | bytes 1081348 | tf_op jit(solution)/shard_map/while/body/eval_jaxpr/reduce_sum | solution.py:23
  30.2 4.0 %fusion.235 = bf16[4096,128]{1,0:T(8,128)(2,1)S(1)} fusion(bf16[512,128]{1,0:T(8,128)(2,1)S(1)} %get-tuple-element.715, bf16[128,512]{1,0:T(8,128)(2,1)S(1)} %get-tuple-element.714, f32[128]{0:T(128)S(1)} %get-tuple-element.713, f32[4096]{0:T(1024)S(1)} %add_rsqrt_fusion.8, f32[4096]{0:T(1024)S(1)} %broadcast_multiply_fusion.8, ...), kind=kOutput, calls=%fused_computation.61.clone.1 | convolution fusion | flops 1082130432 | bytes 3442176 | tf_op jit(solution)/shard_map/while/body/eval_jaxpr/dot_general | solution.py:28
  35.9 1.6 convert_reduce_fusion.8
  37.5 2.3 %fusion.234 = f32[4096]{0:T(1024)S(1)} fusion(f32[4096]{0:T(1024)S(1)} %broadcast_multiply_fusion.8, bf16[4,4096,128]{2,1,0:T(8,128)(2,1)} %get-tuple-element.712, s32[]{:T(128)S(6)} %copy.83), kind=kLoop, calls=%fused_computation.68.clone.1 | loop fusion | flops 2093056 | bytes 1081348 | tf_op jit(solution)/shard_map/while/body/eval_jaxpr/reduce_sum | solution.py:23
  39.8 4.2 %fusion.235 = bf16[4096,128]{1,0:T(8,128)(2,1)S(1)} fusion(bf16[512,128]{1,0:T(8,128)(2,1)S(1)} %get-tuple-element.715, bf16[128,512]{1,0:T(8,128)(2,1)S(1)} %get-tuple-element.714, f32[128]{0:T(128)S(1)} %get-tuple-element.713, f32[4096]{0:T(1024)S(1)} %add_rsqrt_fusion.8, f32[4096]{0:T(1024)S(1)} %broadcast_multiply_fusion.8, ...), kind=kOutput, calls=%fused_computation.61.clone.1 | convolution fusion | flops 1082130432 | bytes 3442176 | tf_op jit(solution)/shard_map/while/body/eval_jaxpr/dot_general | solution.py:28
  45.6 1.6 convert_reduce_fusion.8
  47.2 2.3 %fusion.234 = f32[4096]{0:T(1024)S(1)} fusion(f32[4096]{0:T(1024)S(1)} %broadcast_multiply_fusion.8, bf16[4,4096,128]{2,1,0:T(8,128)(2,1)} %get-tuple-element.712, s32[]{:T(128)S(6)} %copy.83), kind=kLoop, calls=%fused_computation.68.clone.1 | loop fusion | flops 2093056 | bytes 1081348 | tf_op jit(solution)/shard_map/while/body/eval_jaxpr/reduce_sum | solution.py:23
  49.6 4.0 %fusion.235 = bf16[4096,128]{1,0:T(8,128)(2,1)S(1)} fusion(bf16[512,128]{1,0:T(8,128)(2,1)S(1)} %get-tuple-element.715, bf16[128,512]{1,0:T(8,128)(2,1)S(1)} %get-tuple-element.714, f32[128]{0:T(128)S(1)} %get-tuple-element.713, f32[4096]{0:T(1024)S(1)} %add_rsqrt_fusion.8, f32[4096]{0:T(1024)S(1)} %broadcast_multiply_fusion.8, ...), kind=kOutput, calls=%fused_computation.61.clone.1 | convolution fusion | flops 1082130432 | bytes 3442176 | tf_op jit(solution)/shard_map/while/body/eval_jaxpr/dot_general | solution.py:28
  60.1 39.0 %while.42 = (s32[]{:T(128)}, f32[4,4096]{1,0:T(4,128)S(1)}, f32[4,4096]{1,0:T(4,128)S(1)}, bf16[4,4096,128]{2,1,0:T(8,128)(2,1)}, f32[128]{0:T(128)S(1)}, /*inde...) while((s32[]{:T(128)}, f32[4,4096]{1,0:T(4,128)S(1)}, ...), condition=%wide.region_7.8_spmd.clone.clone, body=%wide.region_0.7_spmd.clone.clone.sunk | while | flops 1155256576 | bytes 10046353 | solution.py:131
  60.1 1.6 convert_reduce_fusion.6
  61.7 2.3 %fusion.212 = f32[4096]{0:T(1024)S(1)} fusion(f32[4096]{0:T(1024)S(1)} %broadcast_multiply_fusion.6, bf16[4,4096,128]{2,1,0:T(8,128)(2,1)} %get-tuple-element.748, s32[]{:T(128)S(6)} %copy.92), kind=kLoop, calls=%fused_computation.12.clone.1 | loop fusion | flops 2093056 | bytes 1081348 | tf_op jit(solution)/shard_map/while/body/eval_jaxpr/reduce_sum | solution.py:23
  64.0 4.1 %fusion.213 = bf16[4096,128]{1,0:T(8,128)(2,1)S(1)} fusion(bf16[512,128]{1,0:T(8,128)(2,1)S(1)} %get-tuple-element.751, bf16[128,512]{1,0:T(8,128)(2,1)S(1)} %get-tuple-element.750, f32[128]{0:T(128)S(1)} %get-tuple-element.749, f32[4096]{0:T(1024)S(1)} %add_rsqrt_fusion.6, f32[4096]{0:T(1024)S(1)} %broadcast_multiply_fusion.6, ...), kind=kOutput, calls=%fused_computation.5.clone.1 | convolution fusion | flops 1082130432 | bytes 3442176 | tf_op jit(solution)/shard_map/while/body/eval_jaxpr/dot_general | solution.py:28
  69.8 1.6 convert_reduce_fusion.6
  71.4 2.3 %fusion.212 = f32[4096]{0:T(1024)S(1)} fusion(f32[4096]{0:T(1024)S(1)} %broadcast_multiply_fusion.6, bf16[4,4096,128]{2,1,0:T(8,128)(2,1)} %get-tuple-element.748, s32[]{:T(128)S(6)} %copy.92), kind=kLoop, calls=%fused_computation.12.clone.1 | loop fusion | flops 2093056 | bytes 1081348 | tf_op jit(solution)/shard_map/while/body/eval_jaxpr/reduce_sum | solution.py:23
  73.7 4.1 %fusion.213 = bf16[4096,128]{1,0:T(8,128)(2,1)S(1)} fusion(bf16[512,128]{1,0:T(8,128)(2,1)S(1)} %get-tuple-element.751, bf16[128,512]{1,0:T(8,128)(2,1)S(1)} %get-tuple-element.750, f32[128]{0:T(128)S(1)} %get-tuple-element.749, f32[4096]{0:T(1024)S(1)} %add_rsqrt_fusion.6, f32[4096]{0:T(1024)S(1)} %broadcast_multiply_fusion.6, ...), kind=kOutput, calls=%fused_computation.5.clone.1 | convolution fusion | flops 1082130432 | bytes 3442176 | tf_op jit(solution)/shard_map/while/body/eval_jaxpr/dot_general | solution.py:28
  81.1 2.3 %fusion.212 = f32[4096]{0:T(1024)S(1)} fusion(f32[4096]{0:T(1024)S(1)} %broadcast_multiply_fusion.6, bf16[4,4096,128]{2,1,0:T(8,128)(2,1)} %get-tuple-element.748, s32[]{:T(128)S(6)} %copy.92), kind=kLoop, calls=%fused_computation.12.clone.1 | loop fusion | flops 2093056 | bytes 1081348 | tf_op jit(solution)/shard_map/while/body/eval_jaxpr/reduce_sum | solution.py:23
  83.4 4.2 %fusion.213 = bf16[4096,128]{1,0:T(8,128)(2,1)S(1)} fusion(bf16[512,128]{1,0:T(8,128)(2,1)S(1)} %get-tuple-element.751, bf16[128,512]{1,0:T(8,128)(2,1)S(1)} %get-tuple-element.750, f32[128]{0:T(128)S(1)} %get-tuple-element.749, f32[4096]{0:T(1024)S(1)} %add_rsqrt_fusion.6, f32[4096]{0:T(1024)S(1)} %broadcast_multiply_fusion.6, ...), kind=kOutput, calls=%fused_computation.5.clone.1 | convolution fusion | flops 1082130432 | bytes 3442176 | tf_op jit(solution)/shard_map/while/body/eval_jaxpr/dot_general | solution.py:28
  89.2 1.6 convert_reduce_fusion.6
  90.8 2.3 %fusion.212 = f32[4096]{0:T(1024)S(1)} fusion(f32[4096]{0:T(1024)S(1)} %broadcast_multiply_fusion.6, bf16[4,4096,128]{2,1,0:T(8,128)(2,1)} %get-tuple-element.748, s32[]{:T(128)S(6)} %copy.92), kind=kLoop, calls=%fused_computation.12.clone.1 | loop fusion | flops 2093056 | bytes 1081348 | tf_op jit(solution)/shard_map/while/body/eval_jaxpr/reduce_sum | solution.py:23
  93.2 4.2 %fusion.213 = bf16[4096,128]{1,0:T(8,128)(2,1)S(1)} fusion(bf16[512,128]{1,0:T(8,128)(2,1)S(1)} %get-tuple-element.751, bf16[128,512]{1,0:T(8,128)(2,1)S(1)} %get-tuple-element.750, f32[128]{0:T(128)S(1)} %get-tuple-element.749, f32[4096]{0:T(1024)S(1)} %add_rsqrt_fusion.6, f32[4096]{0:T(1024)S(1)} %broadcast_multiply_fusion.6, ...), kind=kOutput, calls=%fused_computation.5.clone.1 | convolution fusion | flops 1082130432 | bytes 3442176 | tf_op jit(solution)/shard_map/while/body/eval_jaxpr/dot_general | solution.py:28
  100.0 38.7 %while.43 = (s32[]{:T(128)}, f32[4,4096]{1,0:T(4,128)S(1)}, f32[4,4096]{1,0:T(4,128)S(1)}, bf16[4,4096,128]{2,1,0:T(8,128)(2,1)}, f32[128]{0:T(128)S(1)}, /*inde...) while((s32[]{:T(128)}, f32[4,4096]{1,0:T(4,128)S(1)}, ...), condition=%wide.region_15.16_spmd.clone.clone, body=%wide.region_8.15_spmd.clone.clone.sunk | while | flops 1155256576 | bytes 10046353 | solution.py:131
  101.6 2.3 %fusion.223 = f32[4096]{0:T(1024)S(1)} fusion(f32[4096]{0:T(1024)S(1)} %broadcast_multiply_fusion.7, bf16[4,4096,128]{2,1,0:T(8,128)(2,1)} %get-tuple-element.784, s32[]{:T(128)S(6)} %copy.101), kind=kLoop, calls=%fused_computation.40.clone.1 | loop fusion | flops 2093056 | bytes 1081348 | tf_op jit(solution)/shard_map/while/body/eval_jaxpr/reduce_sum | solution.py:23
  103.9 4.0 %fusion.224 = bf16[4096,128]{1,0:T(8,128)(2,1)S(1)} fusion(bf16[512,128]{1,0:T(8,128)(2,1)S(1)} %get-tuple-element.787, bf16[128,512]{1,0:T(8,128)(2,1)S(1)} %get-tuple-element.786, f32[128]{0:T(128)S(1)} %get-tuple-element.785, f32[4096]{0:T(1024)S(1)} %add_rsqrt_fusion.7, f32[4096]{0:T(1024)S(1)} %broadcast_multiply_fusion.7, ...), kind=kOutput, calls=%fused_computation.33.clone.1 | convolution fusion | flops 1082130432 | bytes 3442176 | tf_op jit(solution)/shard_map/while/body/eval_jaxpr/dot_general | solution.py:28
  109.6 1.6 convert_reduce_fusion.7
  111.2 2.3 %fusion.223 = f32[4096]{0:T(1024)S(1)} fusion(f32[4096]{0:T(1024)S(1)} %broadcast_multiply_fusion.7, bf16[4,4096,128]{2,1,0:T(8,128)(2,1)} %get-tuple-element.784, s32[]{:T(128)S(6)} %copy.101), kind=kLoop, calls=%fused_computation.40.clone.1 | loop fusion | flops 2093056 | bytes 1081348 | tf_op jit(solution)/shard_map/while/body/eval_jaxpr/reduce_sum | solution.py:23
  113.5 4.0 %fusion.224 = bf16[4096,128]{1,0:T(8,128)(2,1)S(1)} fusion(bf16[512,128]{1,0:T(8,128)(2,1)S(1)} %get-tuple-element.787, bf16[128,512]{1,0:T(8,128)(2,1)S(1)} %get-tuple-element.786, f32[128]{0:T(128)S(1)} %get-tuple-element.785, f32[4096]{0:T(1024)S(1)} %add_rsqrt_fusion.7, f32[4096]{0:T(1024)S(1)} %broadcast_multiply_fusion.7, ...), kind=kOutput, calls=%fused_computation.33.clone.1 | convolution fusion | flops 1082130432 | bytes 3442176 | tf_op jit(solution)/shard_map/while/body/eval_jaxpr/dot_general | solution.py:28
  119.2 1.6 convert_reduce_fusion.7
  120.8 2.3 %fusion.223 = f32[4096]{0:T(1024)S(1)} fusion(f32[4096]{0:T(1024)S(1)} %broadcast_multiply_fusion.7, bf16[4,4096,128]{2,1,0:T(8,128)(2,1)} %get-tuple-element.784, s32[]{:T(128)S(6)} %copy.101), kind=kLoop, calls=%fused_computation.40.clone.1 | loop fusion | flops 2093056 | bytes 1081348 | tf_op jit(solution)/shard_map/while/body/eval_jaxpr/reduce_sum | solution.py:23
  123.2 4.0 %fusion.224 = bf16[4096,128]{1,0:T(8,128)(2,1)S(1)} fusion(bf16[512,128]{1,0:T(8,128)(2,1)S(1)} %get-tuple-element.787, bf16[128,512]{1,0:T(8,128)(2,1)S(1)} %get-tuple-element.786, f32[128]{0:T(128)S(1)} %get-tuple-element.785, f32[4096]{0:T(1024)S(1)} %add_rsqrt_fusion.7, f32[4096]{0:T(1024)S(1)} %broadcast_multiply_fusion.7, ...), kind=kOutput, calls=%fused_computation.33.clone.1 | convolution fusion | flops 1082130432 | bytes 3442176 | tf_op jit(solution)/shard_map/while/body/eval_jaxpr/dot_general | solution.py:28
  130.4 2.3 %fusion.223 = f32[4096]{0:T(1024)S(1)} fusion(f32[4096]{0:T(1024)S(1)} %broadcast_multiply_fusion.7, bf16[4,4096,128]{2,1,0:T(8,128)(2,1)} %get-tuple-element.784, s32[]{:T(128)S(6)} %copy.101), kind=kLoop, calls=%fused_computation.40.clone.1 | loop fusion | flops 2093056 | bytes 1081348 | tf_op jit(solution)/shard_map/while/body/eval_jaxpr/reduce_sum | solution.py:23
  132.7 4.1 %fusion.224 = bf16[4096,128]{1,0:T(8,128)(2,1)S(1)} fusion(bf16[512,128]{1,0:T(8,128)(2,1)S(1)} %get-tuple-element.787, bf16[128,512]{1,0:T(8,128)(2,1)S(1)} %get-tuple-element.786, f32[128]{0:T(128)S(1)} %get-tuple-element.785, f32[4096]{0:T(1024)S(1)} %add_rsqrt_fusion.7, f32[4096]{0:T(1024)S(1)} %broadcast_multiply_fusion.7, ...), kind=kOutput, calls=%fused_computation.33.clone.1 | convolution fusion | flops 1082130432 | bytes 3442176 | tf_op jit(solution)/shard_map/while/body/eval_jaxpr/dot_general | solution.py:28
  140.8 4.2 %all-to-all-start = ((f32[4,128,128]{2,1,0:T(8,128)}), f32[4,128,128]{2,1,0:T(8,128)S(1)}, u32[]{:S(2)}, u32[]{:S(2)}) async-start(f32[4,128,128]{2,1,0:T(8,128)} %copy.41), calls=%async_computation | async-start | bytes 524288 | tf_op jit(solution)/shard_map/all_to_all | solution.py:147
  147.3 3.7 %all-to-all-done = f32[4,128,128]{2,1,0:T(8,128)S(1)} async-done(((f32[4,128,128]{2,1,0:T(8,128)}), f32[4,128,128]{2,1,0:T(8,128)S(1)}, u32[]{:S(2)}, u32[]{:S(2)}) %all-to-all-start) | async-done | bytes 262176 | tf_op jit(solution)/shard_map/all_to_all | solution.py:147
  151.1 3.4 %all-to-all-start.2 = ((f32[4,128,128]{2,1,0:T(8,128)}), f32[4,128,128]{2,1,0:T(8,128)S(1)}, u32[]{:S(2)}, u32[]{:S(2)}) async-start(f32[4,128,128]{2,1,0:T(8,128)} %copy.51), calls=%async_computation.2 | async-start | bytes 524288 | tf_op jit(solution)/shard_map/all_to_all | solution.py:148
  156.7 3.8 %all-to-all-done.2 = f32[4,128,128]{2,1,0:T(8,128)S(1)} async-done(((f32[4,128,128]{2,1,0:T(8,128)}), f32[4,128,128]{2,1,0:T(8,128)S(1)}, u32[]{:S(2)}, u32[]{:S(2)}) %all-to-all-start.2) | async-done | bytes 262176 | tf_op jit(solution)/shard_map/all_to_all | solution.py:148
  160.4 6.4 %all-to-all-start.1 = ((f32[8,3,64,128]{3,2,1,0:T(8,128)}), f32[8,3,64,128]{3,2,1,0:T(8,128)S(1)}, u32[]{:S(2)}, u32[]{:S(2)}) async-start(f32[8,3,64,128]{3,2,1,0:T(8,128)} %copy.46), calls=%async_computation.1 | async-start | bytes 1572864 | tf_op jit(solution)/shard_map/all_to_all | solution.py:194
  168.0 2.1 collective-permute-start
  172.3 2.9 %collective-permute-start.3 = (f32[1,3,64]{2,0,1:T(1,128)S(1)}, f32[1,3,64]{2,0,1:T(1,128)S(1)}, u32[]{:S(2)}, u32[]{:S(2)}) collective-permute-start(f32[1,3,64]{2,0,1:T(1,128)S(1)} %get-tuple-element.442), channel_id=1, source_target_pairs={{0,16},{4,20},{8,24},{12,28},{16,0},{20,4},{24,8},{28,12},{1,17},{... | collective-permute-start | bytes 2312 | tf_op jit(solution)/shard_map/ppermute | solution.py:189
  176.7 3.3 %collective-permute-start.5 = (f32[1,3,64]{2,0,1:T(1,128)S(1)}, f32[1,3,64]{2,0,1:T(1,128)S(1)}, u32[]{:S(2)}, u32[]{:S(2)}) collective-permute-start(f32[1,3,64]{2,0,1:T(1,128)S(1)} %get-tuple-element.440), channel_id=1, source_target_pairs={{0,24},{4,28},{8,16},{12,20},{16,8},{20,12},{24,0},{28,4},{1,25},{... | collective-permute-start | bytes 2312 | tf_op jit(solution)/shard_map/ppermute | solution.py:189
  179.9 4.2 %collective-permute-start.6 = (f32[1,3,64]{2,0,1:T(1,128)S(1)}, f32[1,3,64]{2,0,1:T(1,128)S(1)}, u32[]{:S(2)}, u32[]{:S(2)}) collective-permute-start(f32[1,3,64]{2,0,1:T(1,128)S(1)} %get-tuple-element.439), channel_id=1, source_target_pairs={{0,28},{4,24},{8,20},{12,16},{16,12},{20,8},{24,4},{28,0},{1,29},{... | collective-permute-start | bytes 2312 | tf_op jit(solution)/shard_map/ppermute | solution.py:189
  184.4 2.7 %collective-permute-done.3 = f32[1,3,64]{2,0,1:T(1,128)S(1)} collective-permute-done((f32[1,3,64]{2,0,1:T(1,128)S(1)}, f32[1,3,64]{2,0,1:T(1,128)S(1)}, u32[]{:S(2)}, u32[]{:S(2)}) %collective-permute-start.3) | collective-permute-done | bytes 800 | tf_op jit(solution)/shard_map/ppermute | solution.py:189
  192.2 20.2 %pmax.7 = f32[1]{0:T(128)} all-reduce(f32[1]{0:T(128)} %bitcast.60), channel_id=1, replica_groups=mesh['tile'=8,'cplx'=4] {'tile'}, use_global_device_ids=true, to_apply=%region_32.33 | all-reduce | flops 1 | bytes 8 | tf_op jit(solution)/shard_map/pmax | solution.py:220
  (188 shorter events, 43.4 us)
Async XLA Ops:
  6.1 9.0 %copy-start.3 = (s32[4]{0:T(128)S(1)}, s32[4]{0:T(128)}, u32[]{:S(2)}) copy-start(s32[4]{0:T(128)} %param.17) | copy-start | bytes 52
  6.1 10.3 %copy-start = (bf16[128,64]{0,1:T(8,128)(2,1)S(1)}, bf16[128,64]{0,1:T(8,128)(2,1)}, u32[]{:S(2)}) copy-start(bf16[128,64]{0,1:T(8,128)(2,1)} %param.22) | copy-start | bytes 49156
  6.2 10.3 %copy-start.1 = (f32[64]{0:T(128)S(1)}, f32[64]{0:T(128)}, u32[]{:S(2)}) copy-start(f32[64]{0:T(128)} %param.23) | copy-start | bytes 772
  6.2 10.3 %copy-start.4 = (bf16[128,512]{1,0:T(8,128)(2,1)S(1)}, bf16[128,512]{1,0:T(8,128)(2,1)}, u32[]{:S(2)}) copy-start(bf16[128,512]{1,0:T(8,128)(2,1)} %param.20) | copy-start | bytes 393220
  6.2 10.3 %copy-start.5 = (bf16[512,128]{1,0:T(8,128)(2,1)S(1)}, bf16[512,128]{1,0:T(8,128)(2,1)}, u32[]{:S(2)}) copy-start(bf16[512,128]{1,0:T(8,128)(2,1)} %param.21) | copy-start | bytes 393220
  6.2 10.3 %copy-start.6 = (f32[128]{0:T(128)S(1)}, f32[128]{0:T(128)}, u32[]{:S(2)}) copy-start(f32[128]{0:T(128)} %param.19) | copy-start | bytes 1540
  16.5 38.8 %copy-start.2 = (s32[4,512]{1,0:T(4,128)S(1)}, s32[4,512]{1,0:T(4,128)}, u32[]{:S(2)}) copy-start(s32[4,512]{1,0:T(4,128)} %param.18) | copy-start | bytes 24580
  140.8 10.2 %all-to-all-start = ((f32[4,128,128]{2,1,0:T(8,128)}), f32[4,128,128]{2,1,0:T(8,128)S(1)}, u32[]{:S(2)}, u32[]{:S(2)}) async-start(f32[4,128,128]{2,1,0:T(8,128)} %copy.41), calls=%async_computation | async-start | bytes 524288 | tf_op jit(solution)/shard_map/all_to_all | solution.py:147
  151.1 9.4 %all-to-all-start.2 = ((f32[4,128,128]{2,1,0:T(8,128)}), f32[4,128,128]{2,1,0:T(8,128)S(1)}, u32[]{:S(2)}, u32[]{:S(2)}) async-start(f32[4,128,128]{2,1,0:T(8,128)} %copy.51), calls=%async_computation.2 | async-start | bytes 524288 | tf_op jit(solution)/shard_map/all_to_all | solution.py:148
  160.4 27.5 %all-to-all-start.1 = ((f32[8,3,64,128]{3,2,1,0:T(8,128)}), f32[8,3,64,128]{3,2,1,0:T(8,128)S(1)}, u32[]{:S(2)}, u32[]{:S(2)}) async-start(f32[8,3,64,128]{3,2,1,0:T(8,128)} %copy.46), calls=%async_computation.1 | async-start | bytes 1572864 | tf_op jit(solution)/shard_map/all_to_all | solution.py:194
  168.0 8.7 %collective-permute-start = (f32[1,3,64]{2,0,1:T(1,128)S(1)}, f32[1,3,64]{2,0,1:T(1,128)S(1)}, u32[]{:S(2)}, u32[]{:S(2)}) collective-permute-start(f32[1,3,64]{2,0,1:T(1,128)S(1)} %get-tuple-element.445), channel_id=1, source_target_pairs={{0,4},{4,0},{8,12},{12,8},{16,20},{20,16},{24,28},{28,24},{1,5},{5... | collective-permute-start | bytes 2312 | tf_op jit(solution)/shard_map/ppermute | solution.py:189
  170.1 9.8 %collective-permute-start.1 = (f32[1,3,64]{2,0,1:T(1,128)S(1)}, f32[1,3,64]{2,0,1:T(1,128)S(1)}, u32[]{:S(2)}, u32[]{:S(2)}) collective-permute-start(f32[1,3,64]{2,0,1:T(1,128)S(1)} %get-tuple-element.444), channel_id=1, source_target_pairs={{0,8},{4,12},{8,0},{12,4},{16,24},{20,28},{24,16},{28,20},{1,9},{5... | collective-permute-start | bytes 2312 | tf_op jit(solution)/shard_map/ppermute | solution.py:189
  172.3 12.0 %collective-permute-start.2 = (f32[1,3,64]{2,0,1:T(1,128)S(1)}, f32[1,3,64]{2,0,1:T(1,128)S(1)}, u32[]{:S(2)}, u32[]{:S(2)}) collective-permute-start(f32[1,3,64]{2,0,1:T(1,128)S(1)} %get-tuple-element.443), channel_id=1, source_target_pairs={{0,12},{4,8},{8,4},{12,0},{16,28},{20,24},{24,20},{28,16},{1,13},{... | collective-permute-start | bytes 2312 | tf_op jit(solution)/shard_map/ppermute | solution.py:189
  172.3 14.8 %collective-permute-start.3 = (f32[1,3,64]{2,0,1:T(1,128)S(1)}, f32[1,3,64]{2,0,1:T(1,128)S(1)}, u32[]{:S(2)}, u32[]{:S(2)}) collective-permute-start(f32[1,3,64]{2,0,1:T(1,128)S(1)} %get-tuple-element.442), channel_id=1, source_target_pairs={{0,16},{4,20},{8,24},{12,28},{16,0},{20,4},{24,8},{28,12},{1,17},{... | collective-permute-start | bytes 2312 | tf_op jit(solution)/shard_map/ppermute | solution.py:189
  175.2 12.6 %collective-permute-start.4 = (f32[1,3,64]{2,0,1:T(1,128)S(1)}, f32[1,3,64]{2,0,1:T(1,128)S(1)}, u32[]{:S(2)}, u32[]{:S(2)}) collective-permute-start(f32[1,3,64]{2,0,1:T(1,128)S(1)} %get-tuple-element.441), channel_id=1, source_target_pairs={{0,20},{4,16},{8,28},{12,24},{16,4},{20,0},{24,12},{28,8},{1,21},{... | collective-permute-start | bytes 2312 | tf_op jit(solution)/shard_map/ppermute | solution.py:189
  176.7 11.2 %collective-permute-start.5 = (f32[1,3,64]{2,0,1:T(1,128)S(1)}, f32[1,3,64]{2,0,1:T(1,128)S(1)}, u32[]{:S(2)}, u32[]{:S(2)}) collective-permute-start(f32[1,3,64]{2,0,1:T(1,128)S(1)} %get-tuple-element.440), channel_id=1, source_target_pairs={{0,24},{4,28},{8,16},{12,20},{16,8},{20,12},{24,0},{28,4},{1,25},{... | collective-permute-start | bytes 2312 | tf_op jit(solution)/shard_map/ppermute | solution.py:189
  179.9 8.0 %collective-permute-start.6 = (f32[1,3,64]{2,0,1:T(1,128)S(1)}, f32[1,3,64]{2,0,1:T(1,128)S(1)}, u32[]{:S(2)}, u32[]{:S(2)}) collective-permute-start(f32[1,3,64]{2,0,1:T(1,128)S(1)} %get-tuple-element.439), channel_id=1, source_target_pairs={{0,28},{4,24},{8,20},{12,16},{16,12},{20,8},{24,4},{28,0},{1,29},{... | collective-permute-start | bytes 2312 | tf_op jit(solution)/shard_map/ppermute | solution.py:189
